TPU v7x, 32 devices: a whole 2x2x4 slice. The times are simulated.
32 devices in a mesh: batch: 8 (over z, y), seq: 4 (over x, core).
Axes of the slice: x: 2, y: 2, z: 4, core: 2. Of those that a mesh axis runs over, the one named last changes fastest.
Arguments:
- forward_embed: bfloat16 [12288, 1536], P(('batch', 'seq')), parts along dimension 0, may hold values from -6 to 6
- reverse_embed: bfloat16 [12288, 1536], P(('batch', 'seq')), parts along dimension 0, may hold values from -6 to 6
- conv_weight: bfloat16 [1, 3, 1536, 1536], P(None, None, 'seq'), may hold values from -0.09375 to 0.09375
- conv_bias: float32 [1, 1536], replicated, may hold values from -0.5 to 0.5
- head_weight: bfloat16 [1536, 1024], replicated, may hold values from -0.15625 to 0.15625
- head_bias: float32 [1024], replicated, may hold values from -1 to 1
Outputs:
- averaged: bfloat16 [12288, 1024], P(('batch', 'seq')), parts along dimension 0
There are 8 independent parts, one for each index of `batch`. A program takes and returns all parts, laid end to end along the dimension named above; an argument that names none is the same for every part. Nothing has to cross between parts.
All inputs are finite; a program needn't handle non-finite values.
Results may differ from a plain program's by a relative error of at most 0.008.
Values may be sent and summed in bfloat16 or wider, within the bound.
A program may use at most 128 MiB of HBM per device.

v0:
```python
import jax
import jax.numpy as jnp
from jax import lax
from jax.sharding import PartitionSpec as P


def with_halo(block, sides, width):
    for axis, dim in sides:
        count = lax.axis_size(axis)
        forward = [(i, i + 1) for i in range(count - 1)]
        backward = [(target, source) for source, target in forward]
        low = lax.ppermute(
            lax.slice_in_dim(block, block.shape[dim] - width, None, axis=dim), axis, forward
        )
        high = lax.ppermute(lax.slice_in_dim(block, 0, width, axis=dim), axis, backward)
        block = jnp.concatenate([low, block, high], axis=dim)
    return block


def partner(block, axis, stride):
    count = lax.axis_size(axis)
    route = []
    for low in range(count):
        high = low | 1 << stride
        if high != low and high < count:
            route += [(low, high), (high, low)]
    return lax.ppermute(block, axis, route)


def convolve(stacked, flips, kernel, bias):
    count = stacked.shape[1]
    padded = with_halo(stacked, (("seq", 1),), 1)
    empty = jnp.zeros((stacked.shape[0], count, kernel.shape[2]), jnp.float32)
    piece = lax.all_gather(kernel, "seq", axis=1, tiled=True)
    taps = piece[::-1] if flips[0] else piece
    term = empty[0]
    for tap in range(3):
        term = term + jnp.dot(
            padded[0, tap : tap + count], taps[tap], preferred_element_type=jnp.float32
        )
    results = [term]
    acc = jnp.stack(results)
    return jax.nn.gelu(acc + bias, approximate=False).astype(jnp.bfloat16)


def run_strands(stacked, flips, conv_weight, conv_bias, head_weight, head_bias):
    hidden = stacked
    hidden = convolve(hidden, flips, conv_weight[0], conv_bias[0])
    logits = (
        jnp.einsum("kbc,ct->kbt", hidden, head_weight, preferred_element_type=jnp.float32)
        + head_bias
    )
    return jax.nn.softplus(logits).astype(jnp.bfloat16)


def per_device(forward_embed, reverse_embed, conv_weight, conv_bias, head_weight, head_bias):
    levels = lax.axis_size("seq").bit_length() - 1
    reverse_input = reverse_embed
    reverse_flip = False
    for level in range(levels):
        reverse_input = partner(reverse_input, "seq", level)
    reverse_input = reverse_input[::-1]
    reverse_flip = True
    forward_tracks = run_strands(
        forward_embed[None], (False,), conv_weight, conv_bias, head_weight, head_bias
    )[0]
    reverse_tracks = run_strands(
        reverse_input[None], (reverse_flip,), conv_weight, conv_bias, head_weight, head_bias
    )[0]
    mean = 0.5 * (forward_tracks.astype(jnp.float32) + reverse_tracks.astype(jnp.float32))
    return mean.astype(jnp.bfloat16)


def solution(mesh):
    return jax.shard_map(
        per_device,
        mesh=mesh,
        in_specs=(
            P(("batch", "seq"), None),
            P(("batch", "seq"), None),
            P(None, None, "seq", None),
            P(),
            P(),
            P(),
        ),
        out_specs=P(("batch", "seq"), None),
        check_vma=False,
    )
```

profile of v0, /device:TPU:0, one launch (start us, length us, event | category | flops | bytes accessed | tf_op | source)
XLA Modules:
  0.0 170.6 jit_solution(10624023718183069302)
XLA Ops:
  6.5 0.0 copy-start
  6.5 0.0 copy-start.2
  6.5 0.0 all-gather.3.cloned.1.call-start
  6.5 0.7 all-gather.3.cloned.1.call-update
  7.3 0.6 collective-permute-start.2
  7.8 2.8 %collective-permute-done.2 = bf16[384,1536]{1,0:T(8,128)(2,1)} collective-permute-done((bf16[384,1536]{1,0:T(8,128)(2,1)}, bf16[384,1536]{1,0:T(8,128)(2,1)}, u32[]{:S(2)}, u32[]{:S(2)}) %collective-permute-start.2) | collective-permute-done | bytes 1179680 | tf_op jit(solution)/shard_map/ppermute | solution.py:27
  10.6 2.8 %collective-permute-start.3 = (bf16[384,1536]{1,0:T(8,128)(2,1)}, bf16[384,1536]{1,0:T(8,128)(2,1)}, u32[]{:S(2)}, u32[]{:S(2)}) collective-permute-start(bf16[384,1536]{1,0:T(8,128)(2,1)} %collective-permute-done.2), channel_id=1, source_target_pairs={{0,2},{2,0},{1,3},{3,1},{4,6},{6,4},{5,7},{7,5},{8,10},{10,8},{9,1... | collective-permute-start | bytes 3538952 | tf_op jit(solution)/shard_map/ppermute | solution.py:27
  13.5 0.8 fusion.114
  14.3 1.3 collective-permute-start.1
  15.6 3.0 %collective-permute-start = (bf16[1,1,1536]{2,1,0:T(2,128)(2,1)S(1)}, bf16[1,1,1536]{2,1,0:T(2,128)(2,1)S(1)}, u32[]{:S(2)}, u32[]{:S(2)}) collective-permute-start(bf16[1,1,1536]{2,1,0:T(2,128)(2,1)S(1)} %get-tuple-element.7), channel_id=1, source_target_pairs={{0,1},{1,2},{2,3},{4,5},{5,6},{6,7},{8,9},{9,10},{10,11},{12,13},{... | collective-permute-start | bytes 9224 | tf_op jit(solution)/shard_map/ppermute | solution.py:12
  18.6 0.0 copy-done.2
  18.6 38.2 %collective-permute-done.3 = bf16[384,1536]{1,0:T(8,128)(2,1)} collective-permute-done((bf16[384,1536]{1,0:T(8,128)(2,1)}, bf16[384,1536]{1,0:T(8,128)(2,1)}, u32[]{:S(2)}, u32[]{:S(2)}) %collective-permute-start.3) | collective-permute-done | bytes 1179680 | tf_op jit(solution)/shard_map/ppermute | solution.py:27
  56.8 17.5 %rev.4 = bf16[384,1536]{1,0:T(8,128)(2,1)} reverse(bf16[384,1536]{1,0:T(8,128)(2,1)} %collective-permute-done.3), dimensions={0} | reverse | bytes 2359296 | tf_op jit(solution)/shard_map/rev | solution.py:62
  74.3 0.8 fusion.113
  75.1 1.3 collective-permute-start.5
  76.4 3.0 %collective-permute-start.4 = (bf16[1,1,1536]{2,1,0:T(2,128)(2,1)S(1)}, bf16[1,1,1536]{2,1,0:T(2,128)(2,1)S(1)}, u32[]{:S(2)}, u32[]{:S(2)}) collective-permute-start(bf16[1,1,1536]{2,1,0:T(2,128)(2,1)S(1)} %get-tuple-element.5), channel_id=1, source_target_pairs={{0,1},{1,2},{2,3},{4,5},{5,6},{6,7},{8,9},{9,10},{10,11},{12,13},{... | collective-permute-start | bytes 9224 | tf_op jit(solution)/shard_map/ppermute | solution.py:12
  79.4 38.6 %all-gather.3.cloned.1.call-done = bf16[1,3,1536,1536]{3,2,1,0:T(8,128)(2,1)} async-done(((bf16[1,3,384,1536]{3,2,1,0:T(8,128)(2,1)}), bf16[1,3,1536,1536]{3,2,1,0:T(8,128)(2,1)}) %all-gather.3.cloned.1.call-update) | async-done | bytes 14155792 | tf_op jit(solution)/shard_map/all_gather | solution.py:34
  118.0 0.0 copy-start.3
  118.0 0.0 copy-start.4
  118.0 6.3 %fusion.3 = f32[384,1536]{1,0:T(8,128)} fusion(bf16[384,1536]{1,0:T(8,128)(2,1)} %param.6, bf16[1,3,1536,1536]{3,2,1,0:T(8,128)(2,1)} %all-gather.3.cloned.1.call-done), kind=kOutput, calls=%fused_computation.8 | convolution fusion | flops 1811939328 | bytes 8257536 | tf_op jit(solution)/shard_map/dot_general | solution.py:38
  124.3 0.0 copy-start.1
  124.3 0.0 collective-permute-done.1
  124.3 0.0 copy-done.3
  124.3 6.4 %fusion.5 = f32[384,1536]{1,0:T(8,128)} fusion(bf16[1,3,1536,1536]{3,2,1,0:T(8,128)(2,1)} %all-gather.3.cloned.1.call-done, bf16[1,1,1536]{2,1,0:T(2,128)(2,1)S(1)} %collective-permute-done.1, bf16[1,384,1536]{2,1,0:T(8,128)(2,1)S(1)} %bitcast.57), kind=kOutput, calls=%fused_computation.10 | convolution fusion | flops 1814298624 | bytes 8260608 | tf_op jit(solution)/shard_map/dot_general | solution.py:38
  130.7 0.0 collective-permute-done.5
  130.7 0.0 copy-done.4
  130.7 0.0 copy-done.1
  130.7 3.4 %fusion = f32[384,1536]{1,0:T(8,128)} fusion(bf16[1,3,1536,1536]{3,2,1,0:T(8,128)(2,1)S(1)} %copy-done.4, bf16[1,1,1536]{2,1,0:T(2,128)(2,1)S(1)} %collective-permute-done.5, bf16[1,384,1536]{2,1,0:T(8,128)(2,1)S(1)} %bitcast.53), kind=kOutput, calls=%fused_computation.5 | convolution fusion | flops 1814298624 | bytes 8263680 | tf_op jit(solution)/shard_map/dot_general | solution.py:38
  134.1 0.0 copy-start.5
  134.1 0.0 collective-permute-done.4
  134.1 3.4 %fusion.4 = f32[384,1536]{1,0:T(8,128)} fusion(bf16[1,3,1536,1536]{3,2,1,0:T(8,128)(2,1)S(1)} %copy-done.4, bf16[1,384,1536]{2,1,0:T(8,128)(2,1)S(1)} %bitcast.54, bf16[1,1,1536]{2,1,0:T(2,128)(2,1)S(1)} %collective-permute-done.4), kind=kOutput, calls=%fused_computation.9 | convolution fusion | flops 1814298624 | bytes 8263680 | tf_op jit(solution)/shard_map/dot_general | solution.py:38
  137.6 0.0 collective-permute-done
  137.6 0.0 copy-done
  137.6 0.0 copy-done.5
  137.6 13.0 %fusion.32 = bf16[384,1024]{1,0:T(8,128)(2,1)} fusion(bf16[1536,1024]{1,0:T(8,128)(2,1)S(1)} %copy-done, f32[384,1536]{1,0:T(8,128)} %fusion.5, f32[384,1536]{1,0:T(8,128)} %fusion.3, bf16[1,3,1536,1536]{3,2,1,0:T(8,128)(2,1)} %all-gather.3.cloned.1.call-done, bf16[1,384,1536]{2,1,0:T(8,128)(2,1)} %bitcast.56, ...), kind=kOutput, calls=%fused_computation.55 | convolution fusion | flops 3065511936 | bytes 14562304 | tf_op jit(solution)/shard_map/kbc,ct->kbt/dot_general | solution.py:50
  150.6 13.1 %multiply_convert_fusion = bf16[384,1024]{1,0:T(8,128)(2,1)} fusion(bf16[384,1024]{1,0:T(8,128)(2,1)} %fusion.32, bf16[1536,1024]{1,0:T(8,128)(2,1)S(1)} %copy-done, f32[384,1536]{1,0:T(8,128)} %fusion, f32[384,1536]{1,0:T(8,128)} %fusion.4, bf16[384,1536]{1,0:T(8,128)(2,1)} %rev.4, bf16[1,3,1536,1536]{3,2,1,0:T(8,128)(2,1)} %all-gather.3.cloned.1.call-done, ...), kind=kOutput, calls=%fused_computation.57 | convolution fusion | flops 3065118720 | bytes 15345664 | tf_op jit(solution)/shard_map/kbc,ct->kbt/dot_general | solution.py:50
  (1 shorter events, 0.0 us)
Async XLA Ops:
  6.5 131.0 %copy-start = (bf16[1536,1024]{1,0:T(8,128)(2,1)S(1)}, bf16[1536,1024]{1,0:T(8,128)(2,1)}, u32[]{:S(2)}) copy-start(bf16[1536,1024]{1,0:T(8,128)(2,1)} %param.10) | copy-start | bytes 9437188
  6.5 12.1 %copy-start.2 = (f32[1,1536]{1,0:T(1,128)S(1)}, f32[1,1536]{1,0:T(1,128)}, u32[]{:S(2)}) copy-start(f32[1,1536]{1,0:T(1,128)} %param.9) | copy-start | bytes 18436
  6.5 111.4 %all-gather.3.cloned.1.call-start = ((), (), s32[]{:S(2)}) async-start(), calls=%async_computation | async-start | bytes 17694720 | tf_op jit(solution)/shard_map/all_gather | solution.py:34
  7.3 3.4 %collective-permute-start.2 = (bf16[384,1536]{1,0:T(8,128)(2,1)}, bf16[384,1536]{1,0:T(8,128)(2,1)}, u32[]{:S(2)}, u32[]{:S(2)}) collective-permute-start(bf16[384,1536]{1,0:T(8,128)(2,1)} %param.7), channel_id=1, source_target_pairs={{0,1},{1,0},{2,3},{3,2},{4,5},{5,4},{6,7},{7,6},{8,9},{9,8},{10,11... | collective-permute-start | bytes 3538952 | tf_op jit(solution)/shard_map/ppermute | solution.py:27
  10.6 46.2 %collective-permute-start.3 = (bf16[384,1536]{1,0:T(8,128)(2,1)}, bf16[384,1536]{1,0:T(8,128)(2,1)}, u32[]{:S(2)}, u32[]{:S(2)}) collective-permute-start(bf16[384,1536]{1,0:T(8,128)(2,1)} %collective-permute-done.2), channel_id=1, source_target_pairs={{0,2},{2,0},{1,3},{3,1},{4,6},{6,4},{5,7},{7,5},{8,10},{10,8},{9,1... | collective-permute-start | bytes 3538952 | tf_op jit(solution)/shard_map/ppermute | solution.py:27
  14.3 110.0 %collective-permute-start.1 = (bf16[1,1,1536]{2,1,0:T(2,128)(2,1)S(1)}, bf16[1,1,1536]{2,1,0:T(2,128)(2,1)S(1)}, u32[]{:S(2)}, u32[]{:S(2)}) collective-permute-start(bf16[1,1,1536]{2,1,0:T(2,128)(2,1)S(1)} %get-tuple-element.8), channel_id=1, source_target_pairs={{1,0},{2,1},{3,2},{5,4},{6,5},{7,6},{9,8},{10,9},{11,10},{13,12},{... | collective-permute-start | bytes 9224 | tf_op jit(solution)/shard_map/ppermute | solution.py:15
  15.6 122.0 %collective-permute-start = (bf16[1,1,1536]{2,1,0:T(2,128)(2,1)S(1)}, bf16[1,1,1536]{2,1,0:T(2,128)(2,1)S(1)}, u32[]{:S(2)}, u32[]{:S(2)}) collective-permute-start(bf16[1,1,1536]{2,1,0:T(2,128)(2,1)S(1)} %get-tuple-element.7), channel_id=1, source_target_pairs={{0,1},{1,2},{2,3},{4,5},{5,6},{6,7},{8,9},{9,10},{10,11},{12,13},{... | collective-permute-start | bytes 9224 | tf_op jit(solution)/shard_map/ppermute | solution.py:12
  75.1 55.6 %collective-permute-start.5 = (bf16[1,1,1536]{2,1,0:T(2,128)(2,1)S(1)}, bf16[1,1,1536]{2,1,0:T(2,128)(2,1)S(1)}, u32[]{:S(2)}, u32[]{:S(2)}) collective-permute-start(bf16[1,1,1536]{2,1,0:T(2,128)(2,1)S(1)} %get-tuple-element.6), channel_id=1, source_target_pairs={{1,0},{2,1},{3,2},{5,4},{6,5},{7,6},{9,8},{10,9},{11,10},{13,12},{... | collective-permute-start | bytes 9224 | tf_op jit(solution)/shard_map/ppermute | solution.py:15
  76.4 57.8 %collective-permute-start.4 = (bf16[1,1,1536]{2,1,0:T(2,128)(2,1)S(1)}, bf16[1,1,1536]{2,1,0:T(2,128)(2,1)S(1)}, u32[]{:S(2)}, u32[]{:S(2)}) collective-permute-start(bf16[1,1,1536]{2,1,0:T(2,128)(2,1)S(1)} %get-tuple-element.5), channel_id=1, source_target_pairs={{0,1},{1,2},{2,3},{4,5},{5,6},{6,7},{8,9},{9,10},{10,11},{12,13},{... | collective-permute-start | bytes 9224 | tf_op jit(solution)/shard_map/ppermute | solution.py:12
  118.0 6.3 %copy-start.3 = (bf16[384,1536]{1,0:T(8,128)(2,1)S(1)}, bf16[384,1536]{1,0:T(8,128)(2,1)}, u32[]{:S(2)}) copy-start(bf16[384,1536]{1,0:T(8,128)(2,1)} %param.6) | copy-start | bytes 3538948
  118.0 12.7 %copy-start.4 = (bf16[1,3,1536,1536]{3,2,1,0:T(8,128)(2,1)S(1)}, bf16[1,3,1536,1536]{3,2,1,0:T(8,128)(2,1)}, u32[]{:S(2)}) copy-start(bf16[1,3,1536,1536]{3,2,1,0:T(8,128)(2,1)} %all-gather.3.cloned.1.call-done) | copy-start | bytes 42467332
  124.3 6.4 %copy-start.1 = (bf16[384,1536]{1,0:T(8,128)(2,1)S(1)}, bf16[384,1536]{1,0:T(8,128)(2,1)}, u32[]{:S(2)}) copy-start(bf16[384,1536]{1,0:T(8,128)(2,1)} %rev.4) | copy-start | bytes 3538948
  134.1 3.4 %copy-start.5 = (f32[1024]{0:T(1024)S(1)}, f32[1024]{0:T(1024)}, u32[]{:S(2)}) copy-start(f32[1024]{0:T(1024)} %param.11) | copy-start | bytes 12292
Sparse Core Ops, SparseCore 0:
  8.9 109.0 all-gather.2
where the time goes:
time: 173 us; the launch traced here: 171 us
  waiting for transfers between devices  80.3 us (46%)
  matrix products  45.7 us (26%)
  local copies, waits for them, and re-layouts  19 us (11%)
  between operations  13.5 us (8%)
  starting transfers between devices  12.1 us (7%)
    ppermute x2, waiting for transfers between devices, partner(): return lax.ppermute(block, axis, route)  41 us
    all_gather x1, waiting for transfers between devices, convolve(): piece = lax.all_gather(kernel, 'seq', axis=1, tiled=True)  38.6 us
    dot_general x2, matrix products, run_strands(): jnp.einsum('kbc,ct->kbt', hidden, head_weight, preferred_element_type=jnp...  26.2 us
    dot_general x4, matrix products, convolve(): jnp.dot(padded[0, tap:tap + count], taps[tap], preferred_element_type=jnp...  19.5 us
    rev x1, local copies, waits for them, and re-layouts, per_device(): reverse_input = reverse_input[::-1]  17.5 us
    ppermute x2, starting transfers between devices, with_halo(): lax.ppermute(lax.slice_in_dim(block, block.shape[dim] - width, None, axis...  6.06 us
  transfers between devices with their start and end apart: 7, of which 3 were waited for; matrix products, arithmetic and copies ran while one was open for 23% of the time, Pallas kernels for 0%

commit v1 on v0

v1 whole, which is shorter than its diff:
```python
import functools
import math

import jax
import jax.numpy as jnp
from jax import lax
from jax.experimental import pallas as pl
from jax.experimental.pallas import tpu as pltpu
from jax.sharding import PartitionSpec as P

MESH = pl.DeviceIdType.MESH
F32 = jnp.float32
BF16 = jnp.bfloat16
UNIT = 128


def gelu(x):
    return (0.5 * x) * (1.0 + lax.erf(x * math.sqrt(0.5)))


def softplus(x):
    u = jnp.exp(-jnp.abs(x))
    return jnp.maximum(x, 0.0) + jnp.where(u < 1e-3, u - 0.5 * u * u, jnp.log(1.0 + u))


def kernel(
    taps, fwd_hbm, rev_hbm, w_hbm, cb_ref, hw_hbm, hb_ref, out_ref,
    embed, halo, xcat, wbuf, acc, headw, logits, flip, sendt, recvt,
    local_sem, halo_send, halo_recv, own_send, own_recv,
    x_send, x_recv, y_send, y_recv, z_send, z_recv, m_send, m_recv, t_send, t_recv,
):
    s = lax.axis_index("seq")
    b = lax.axis_index("batch")
    core = s % 2
    far = s // 2
    mate = s + 1 - 2 * core
    across = s + 2 - 4 * far
    mirror = 3 - s
    shards = (s, mate, across, mirror)
    y = b % 2
    z = (b // 2) % 2
    yp = b + 1 - 2 * y
    zp = b + 2 - 4 * z
    cx = y + (1 - y) * 2 * z
    cy = (1 - y) + y * 2 * z
    cz = 2 * (1 - z)
    rows, channels = embed.shape[1:]
    depth = w_hbm.shape[2]
    units = channels // UNIT
    wide = 2 * UNIT
    blocks = channels // wide
    half = 2 * taps * depth
    tracks = hb_ref.shape[1]
    pieces = tracks // wide

    barrier = pltpu.get_barrier_semaphore()
    for peer in ({"seq": mate}, {"seq": across}, {"seq": mirror}, {"batch": yp}, {"batch": zp}):
        pl.semaphore_signal(barrier, inc=1, device_id=peer, device_id_type=MESH)

    loads = [
        pltpu.make_async_copy(fwd_hbm, embed.at[0], local_sem.at[0]),
        pltpu.make_async_copy(rev_hbm, embed.at[1], local_sem.at[1]),
        pltpu.make_async_copy(hw_hbm, headw, local_sem.at[2]),
    ] + [
        pltpu.make_async_copy(w_hbm.at[0, k], wbuf.at[pl.ds(k * depth, depth)], local_sem.at[3 + k])
        for k in range(taps)
    ]
    for copy in loads:
        copy.start()
    pl.semaphore_wait(barrier, 5)

    def remote(src, dst, send, recv, peer):
        return pltpu.make_async_remote_copy(
            src_ref=src, dst_ref=dst, send_sem=send, recv_sem=recv, device_id=peer, device_id_type=MESH
        )

    tile = halo.shape[2]
    halos = []
    for k, src in enumerate((fwd_hbm, rev_hbm)):
        halos.append(remote(src.at[pl.ds(rows - tile, tile)], halo.at[k, 0], halo_send.at[k, 0], halo_recv.at[k, 0], {"seq": (s + 1) % 4}))
        halos.append(remote(src.at[pl.ds(0, tile)], halo.at[k, 1], halo_send.at[k, 1], halo_recv.at[k, 1], {"seq": (s + 3) % 4}))
    for copy in halos:
        copy.start()

    def cell(slot, tap, unit):
        row = pl.multiple_of((slot * taps + tap) * depth, depth)
        return wbuf.at[pl.ds(row, depth), pl.ds(pl.multiple_of(unit * UNIT, UNIT), UNIT)]

    def x_copy(j):
        src = w_hbm.at[0, cx, :, pl.ds(pl.multiple_of(j * UNIT, UNIT), UNIT)]
        return remote(src, cell(2, cx, j), x_send.at[j], x_recv.at[j], {"seq": across})

    def y_copy(color, j):
        return remote(cell(2, color, j), cell(2, color, j), y_send.at[j], y_recv.at[j], {"batch": yp})

    def z_copy(color, j):
        return remote(cell(2, color, j), cell(2, color, j), z_send.at[j], z_recv.at[j], {"batch": zp})

    def m_copy(kind, color, j):
        return remote(cell(2, color, j), cell(3, color, j), m_send.at[kind, j], m_recv.at[kind, j], {"seq": mate})

    own = [
        remote(w_hbm.at[0, k], wbuf.at[pl.ds((taps + k) * depth, depth)], own_send.at[k], own_recv.at[k], {"seq": mate})
        for k in range(taps)
    ]

    def start_x(j, c):
        x_copy(j).start()
        return c

    lax.fori_loop(0, units, start_x, 0)
    for copy in own:
        copy.start()

    r = lax.broadcasted_iota(jnp.int32, (rows, rows), 0)
    c = lax.broadcasted_iota(jnp.int32, (rows, rows), 1)
    flip[...] = jnp.where(r + c == rows - 1, 1.0, 0.0).astype(BF16)

    for copy in loads[:2]:
        copy.wait()
    for copy in halos:
        copy.wait()
    line = lax.broadcasted_iota(jnp.int32, (rows, depth), 0)
    for k in range(2):
        for slot in range(4):
            cols = pl.ds(pl.multiple_of(shards[slot] * depth, UNIT), depth)
            mid = embed[k, :, cols]
            wide_mid = mid.astype(F32)
            low = halo[k, 0, :, cols].astype(F32)[tile - 1 : tile]
            high = halo[k, 1, :, cols].astype(F32)[0:1]
            low = jnp.where(s == 0, 0.0, low)
            high = jnp.where(s == 3, 0.0, high)
            before = jnp.where(line == 0, low, pltpu.roll(wide_mid, 1, 0))
            after = jnp.where(line == rows - 1, high, pltpu.roll(wide_mid, rows - 1, 0))
            for tap, part in enumerate((before.astype(BF16), mid, after.astype(BF16))):
                xcat[k, :, pl.ds((slot * taps + tap) * depth, depth)] = part

    def near(m):
        cols = pl.ds(pl.multiple_of(m * wide, wide), wide)
        w = wbuf[pl.ds(0, half), cols]
        for k in range(2):
            acc[k, :, cols] = jnp.dot(xcat[k, :, pl.ds(0, half)], w, preferred_element_type=F32) + cb_ref[:, cols]

    def remote_part(k, m):
        cols = pl.ds(pl.multiple_of(m * wide, wide), wide)
        total = acc[k, :, cols] + jnp.dot(
            xcat[k, :, pl.ds(half, half)], wbuf[pl.ds(half, half), cols], preferred_element_type=F32
        )
        hidden = gelu(total).astype(BF16)
        logits[k] = logits[k] + jnp.dot(hidden, headw[cols, :], preferred_element_type=F32)

    for copy in loads[2:]:
        copy.wait()
    for copy in own:
        copy.wait()
    for k in range(2):
        logits[k] = jnp.broadcast_to(hb_ref[...], (rows, tracks))
    lead = 2

    def first(m, carry):
        near(m)
        return carry

    lax.fori_loop(0, lead, first, 0)

    def step(j, carry):
        @pl.when(j < units)
        def _():
            x_copy(j).wait_recv()
            y_copy(cx, j).start()

            @pl.when(y == 0)
            def _():
                z_copy(cx, j).start()

            m_copy(0, cx, j).start()

        @pl.when((j >= 1) & (j < units + 1))
        def _():
            y_copy(cy, j - 1).wait_recv()

            @pl.when(y == 1)
            def _():
                z_copy(cy, j - 1).start()

            m_copy(1, cy, j - 1).start()

        @pl.when((j >= 2) & (j < units + 2))
        def _():
            z_copy(cz, j - 2).wait_recv()
            m_copy(2, cz, j - 2).start()

        @pl.when(j < blocks - lead)
        def _():
            near(j + lead)

        @pl.when(j >= 4)
        def _():
            k = (j + 1) % 2
            m = (j - 4) // 2

            @pl.when(k == 1)
            def _():
                for kind, color in enumerate((cx, cy, cz)):
                    m_copy(kind, color, 2 * m).wait_recv()
                    m_copy(kind, color, 2 * m + 1).wait_recv()

            remote_part(k, m)

        return carry

    lax.fori_loop(0, 2 * blocks + 3, step, 0)

    def t_copy(p):
        cols = pl.ds(p * wide, wide)
        return remote(sendt.at[:, cols], recvt.at[:, cols], t_send.at[p], t_recv.at[p], {"seq": mirror})

    for p in range(pieces):
        cols = pl.ds(p * wide, wide)
        value = softplus(logits[1, :, cols]).astype(BF16)
        sendt[:, cols] = jnp.dot(flip[...], value, preferred_element_type=F32).astype(BF16)
        if p:
            t_copy(p - 1).start()
    remote_part(0, blocks - 1)
    t_copy(pieces - 1).start()
    for p in range(pieces):
        cols = pl.ds(p * wide, wide)
        logits[0, :, cols] = softplus(logits[0, :, cols]).astype(BF16).astype(F32)
    for p in range(pieces):
        cols = pl.ds(p * wide, wide)
        t_copy(p).wait_recv()
        out_ref[:, cols] = (0.5 * (logits[0, :, cols] + recvt[:, cols].astype(F32))).astype(BF16)

    def drain(j, carry):
        x_copy(j).wait_send()
        y_copy(cx, j).wait_send()
        z_copy(2 * z, j).wait_send()
        for kind, color in enumerate((cx, cy, cz)):
            m_copy(kind, color, j).wait_send()
        return carry

    lax.fori_loop(0, units, drain, 0)
    for p in range(pieces):
        t_copy(p).wait_send()


def fused(forward_embed, reverse_embed, conv_weight, conv_bias, head_weight, head_bias):
    rows, channels = forward_embed.shape
    _, taps, depth, _ = conv_weight.shape
    tracks = head_weight.shape[1]
    units = channels // UNIT
    pieces = tracks // (2 * UNIT)
    dma = pltpu.SemaphoreType.DMA
    anywhere = pl.BlockSpec(memory_space=pl.ANY)
    vmem = pl.BlockSpec(memory_space=pltpu.VMEM)
    return pl.pallas_call(
        functools.partial(kernel, taps),
        out_shape=jax.ShapeDtypeStruct((rows, tracks), BF16),
        in_specs=[anywhere, anywhere, anywhere, vmem, anywhere, vmem],
        out_specs=vmem,
        scratch_shapes=[
            pltpu.VMEM((2, rows, channels), BF16),
            pltpu.VMEM((2, 2, 16, channels), BF16),
            pltpu.VMEM((2, rows, 4 * taps * depth), BF16),
            pltpu.VMEM((4 * taps * depth, channels), BF16),
            pltpu.VMEM((2, rows, channels), F32),
            pltpu.VMEM((channels, tracks), BF16),
            pltpu.VMEM((2, rows, tracks), F32),
            pltpu.VMEM((rows, rows), BF16),
            pltpu.VMEM((rows, tracks), BF16),
            pltpu.VMEM((rows, tracks), BF16),
            dma((3 + taps,)),
            dma((2, 2)), dma((2, 2)),
            dma((taps,)), dma((taps,)),
            dma((units,)), dma((units,)),
            dma((units,)), dma((units,)),
            dma((units,)), dma((units,)),
            dma((3, units)), dma((3, units)),
            dma((pieces,)), dma((pieces,)),
        ],
        compiler_params=pltpu.CompilerParams(
            collective_id=0, has_side_effects=True, vmem_limit_bytes=62 * 1024 * 1024
        ),
    )(forward_embed, reverse_embed, conv_weight, conv_bias, head_weight, head_bias[None])


def with_halo(block, axis):
    count = lax.axis_size(axis)
    forward = [(i, i + 1) for i in range(count - 1)]
    backward = [(target, source) for source, target in forward]
    low = lax.ppermute(block[-1:], axis, forward)
    high = lax.ppermute(block[:1], axis, backward)
    return jnp.concatenate([low, block, high], axis=0)


def general(forward_embed, reverse_embed, conv_weight, conv_bias, head_weight, head_bias):
    count = lax.axis_size("seq")
    layers, taps = conv_weight.shape[:2]
    gathered = [lax.all_gather(conv_weight[n], "seq", axis=1, tiled=True) for n in range(layers)]

    def strand(hidden):
        for n in range(layers):
            rows = hidden.shape[0]
            padded = with_halo(hidden, "seq")
            total = sum(
                jnp.dot(padded[k : k + rows], gathered[n][k], preferred_element_type=F32) for k in range(taps)
            )
            hidden = jax.nn.gelu(total + conv_bias[n], approximate=False).astype(BF16)
        logits = jnp.dot(hidden, head_weight, preferred_element_type=F32) + head_bias
        return jax.nn.softplus(logits).astype(BF16)

    reverse_tracks = strand(reverse_embed)[::-1]
    reverse_tracks = lax.ppermute(reverse_tracks, "seq", [(i, count - 1 - i) for i in range(count)])
    mean = 0.5 * (strand(forward_embed).astype(F32) + reverse_tracks.astype(F32))
    return mean.astype(BF16)


def solution(mesh):
    cubes = mesh.shape["seq"] == 4 and mesh.shape["batch"] % 4 == 0
    return jax.shard_map(
        fused if cubes else general,
        mesh=mesh,
        in_specs=(
            P(("batch", "seq"), None),
            P(("batch", "seq"), None),
            P(None, None, "seq", None),
            P(),
            P(),
            P(),
        ),
        out_specs=P(("batch", "seq"), None),
        check_vma=False,
    )
```

time: 173 us -> 78.5 us (0.45)
  waiting for transfers between devices: 80.3 us -> 0 us
  Pallas kernels: 0 us -> 75.1 us
  matrix products: 45.7 us -> 0 us
  local copies, waits for them, and re-layouts: 19 us -> 2.06 us
  between operations: 13.5 us -> 0.01 us
  starting transfers between devices: 12.1 us -> 0 us
    pallas_call x0 -> x1, Pallas kernels: none -> 75.1 us  [fused(): pl.pallas_call(functools.partial(kernel, taps), out_shape=jax.ShapeDtypeS...]
    dot_general x6 -> x0, matrix products: 45.7 us -> none  [the longest x2 26.2 us: run_strands(): jnp.einsum('kbc,ct->kbt', hidden, head_weight, preferred_element_type=jnp...]
    ppermute x6 -> x0, waiting for transfers between devices: 41 us -> none  [the longest x2 41 us: partner(): return lax.ppermute(block, axis, route)]
    all_gather x1 -> x0, waiting for transfers between devices: 38.6 us -> none  [convolve(): piece = lax.all_gather(kernel, 'seq', axis=1, tiled=True)]
    rev x1 -> x0, local copies, waits for them, and re-layouts: 17.5 us -> none  [per_device(): reverse_input = reverse_input[::-1]]
    ppermute x6 -> x0, starting transfers between devices: 12.1 us -> none  [the longest x2 6.06 us: with_halo(): lax.ppermute(lax.slice_in_dim(block, block.shape[dim] - width, None, axis...]
    unnamed x12 -> x1, local copies, waits for them, and re-layouts: 0.02 us -> 2.06 us
  transfers between devices with their start and end apart: 7 -> 0, of which waited for: 3 -> 0; matrix products, arithmetic and copies ran while one was open for 23% -> 0% of each run, Pallas kernels for 0% -> 0%
where the time goes in v1:
time: 78.5 us; the launch traced here: 77.2 us
  Pallas kernels  75.1 us (96%)
  local copies, waits for them, and re-layouts  2.06 us (3%)
    pallas_call x1, Pallas kernels, fused(): pl.pallas_call(functools.partial(kernel, taps), out_shape=jax.ShapeDtypeS...  75.1 us
    unnamed x1, local copies, waits for them, and re-layouts  2.06 us

profile of v1, /device:TPU:0, one launch (start us, length us, event | category | flops | bytes accessed | tf_op | source)
XLA Modules:
  0.0 77.2 jit_solution(3040231648848998992)
XLA Ops:
  0.0 75.1 %shard_map.64 = bf16[384,1024]{1,0:T(8,128)(2,1)} custom-call(bf16[384,1536]{1,0:T(8,128)(2,1)} %fwd_hbm.1, bf16[384,1536]{1,0:T(8,128)(2,1)} %rev_hbm.1, bf16[1,3,384,1536]{3,2,1,0:T(8,128)(2,1)} %w_hbm.1, f32[1,1536]{1,0:T(1,128)} %cb_ref.1, bf16[1536,1024]{1,0:T(8,128)(2,1)} %hw_hbm.1, f32[1,1024]{1,0:T(1,128)} %bitcast.1), custom_call_target="tpu_custom_call" | custom-call | tf_op jit(solution)/shard_map/pallas_call | solution.py:256
  75.2 2.1 %copy.8 = bf16[384,1024]{1,0:T(8,128)(2,1)} copy(bf16[384,1024]{1,0:T(8,128)(2,1)} %shard_map.64) | data formatting | bytes 1572864

commit v2 on v1

v2 whole, which is shorter than its diff:
```python
import functools
import math

import jax
import jax.numpy as jnp
from jax import lax
from jax.experimental import pallas as pl
from jax.experimental.pallas import tpu as pltpu
from jax.sharding import PartitionSpec as P

MESH = pl.DeviceIdType.MESH
F32 = jnp.float32
BF16 = jnp.bfloat16
LANES = 128
WIDE = 256
SPLIT = 2
LAG = 2


def gelu(x):
    return (0.5 * x) * (1.0 + lax.erf(x * math.sqrt(0.5)))


def softplus(x):
    u = jnp.exp(-jnp.abs(x))
    return jnp.maximum(x, 0.0) + jnp.where(u < 1e-3, u - 0.5 * u * u, jnp.log(1.0 + u))


def kernel(
    taps, fwd_hbm, rev_hbm, w_hbm, cb_ref, hw_hbm, hb_ref, fwd_out, rev_out,
    embed, halo, xcat, wbuf, acc, headw, logits, flip, sendt, keept,
    local_sem, halo_send, halo_recv, own_send, own_recv,
    x_send, x_recv, y_send, y_recv, z_send, z_recv, m_send, m_recv, t_send, t_recv, out_sem,
):
    s = lax.axis_index("seq")
    b = lax.axis_index("batch")
    core = s % 2
    far = s // 2
    mate = s + 1 - 2 * core
    across = s + 2 - 4 * far
    mirror = 3 - s
    shards = (s, mate, across, mirror)
    y = b % 2
    z = (b // 2) % 2
    yp = b + 1 - 2 * y
    zp = b + 2 - 4 * z
    cx = y + (1 - y) * 2 * z
    cy = (1 - y) + y * 2 * z
    cz = 2 * (1 - z)
    rows, channels = embed.shape[1:]
    depth = w_hbm.shape[2]
    wide = WIDE
    blocks = channels // wide
    units = SPLIT * blocks
    part = depth // SPLIT
    half = 2 * taps * depth
    tracks = hb_ref.shape[1]
    pieces = tracks // wide

    barrier = pltpu.get_barrier_semaphore()
    for peer in ({"seq": mate}, {"seq": across}, {"seq": mirror}, {"batch": yp}, {"batch": zp}):
        pl.semaphore_signal(barrier, inc=1, device_id=peer, device_id_type=MESH)

    loads = [
        pltpu.make_async_copy(fwd_hbm, embed.at[0], local_sem.at[0]),
        pltpu.make_async_copy(rev_hbm, embed.at[1], local_sem.at[1]),
        pltpu.make_async_copy(hw_hbm, headw, local_sem.at[2]),
    ] + [
        pltpu.make_async_copy(
            w_hbm.at[0, k, :, pl.ds(m * wide, wide)], wbuf.at[m, pl.ds(k * depth, depth)], local_sem.at[3 + k * blocks + m]
        )
        for m in range(blocks)
        for k in range(taps)
    ]
    for copy in loads:
        copy.start()
    pl.semaphore_wait(barrier, 5)

    def remote(src, dst, send, recv, peer):
        return pltpu.make_async_remote_copy(
            src_ref=src, dst_ref=dst, send_sem=send, recv_sem=recv, device_id=peer, device_id_type=MESH
        )

    tile = halo.shape[2]
    halos = []
    for k, src in enumerate((fwd_hbm, rev_hbm)):
        halos.append(remote(src.at[pl.ds(rows - tile, tile)], halo.at[k, 0], halo_send.at[k, 0], halo_recv.at[k, 0], {"seq": (s + 1) % 4}))
        halos.append(remote(src.at[pl.ds(0, tile)], halo.at[k, 1], halo_send.at[k, 1], halo_recv.at[k, 1], {"seq": (s + 3) % 4}))
    for copy in halos:
        copy.start()

    def cell(slot, tap, unit):
        row = pl.multiple_of((slot * taps + tap) * depth + (unit % SPLIT) * part, 32)
        return wbuf.at[unit // SPLIT, pl.ds(row, part)]

    def x_copy(j):
        row = pl.ds(pl.multiple_of((j % SPLIT) * part, 32), part)
        col = pl.ds(pl.multiple_of((j // SPLIT) * wide, wide), wide)
        return remote(w_hbm.at[0, cx, row, col], cell(2, cx, j), x_send.at[j], x_recv.at[j], {"seq": across})

    def y_copy(color, j):
        return remote(cell(2, color, j), cell(2, color, j), y_send.at[j], y_recv.at[j], {"batch": yp})

    def z_copy(color, j):
        return remote(cell(2, color, j), cell(2, color, j), z_send.at[j], z_recv.at[j], {"batch": zp})

    def m_copy(kind, color, j):
        return remote(cell(2, color, j), cell(3, color, j), m_send.at[kind, j], m_recv.at[kind, j], {"seq": mate})

    own = [
        remote(
            w_hbm.at[0, k, :, pl.ds(m * wide, wide)], wbuf.at[m, pl.ds((taps + k) * depth, depth)],
            own_send.at[k, m], own_recv.at[k, m], {"seq": mate},
        )
        for m in range(blocks)
        for k in range(taps)
    ]

    def start_x(j, c):
        x_copy(j).start()
        return c

    lax.fori_loop(0, units, start_x, 0)
    for copy in own:
        copy.start()

    r = lax.broadcasted_iota(jnp.int32, (rows, rows), 0)
    c = lax.broadcasted_iota(jnp.int32, (rows, rows), 1)
    flip[...] = jnp.where(r + c == rows - 1, 1.0, 0.0).astype(BF16)
    for k in range(2):
        logits[k] = jnp.broadcast_to(hb_ref[...], (rows, tracks))

    line = lax.broadcasted_iota(jnp.int32, (rows, depth), 0)

    def build(k, slot):
        shard = (s // 2 + (slot // 2) * (1 - 2 * far)) * 2 + core + (slot % 2) * (1 - 2 * core)
        cols = pl.ds(pl.multiple_of(shard * depth, LANES), depth)
        mid = embed[k, :, cols]
        wide_mid = mid.astype(F32)
        low = halo[k, 0, :, cols].astype(F32)[tile - 1 : tile]
        high = halo[k, 1, :, cols].astype(F32)[0:1]
        low = jnp.where(s == 0, 0.0, low)
        high = jnp.where(s == 3, 0.0, high)
        before = jnp.where(line == 0, low, pltpu.roll(wide_mid, 1, 0))
        after = jnp.where(line == rows - 1, high, pltpu.roll(wide_mid, rows - 1, 0))
        for tap, value in enumerate((before.astype(BF16), mid, after.astype(BF16))):
            xcat[k, :, pl.ds(pl.multiple_of((slot * taps + tap) * depth, LANES), depth)] = value

    def near(k, m):
        cols = pl.ds(pl.multiple_of(m * wide, wide), wide)
        acc[k, :, cols] = (
            jnp.dot(xcat[k, :, pl.ds(0, half)], wbuf[m, pl.ds(0, half)], preferred_element_type=F32)
            + cb_ref[:, cols]
        )

    def remote_part(k, m):
        cols = pl.ds(pl.multiple_of(m * wide, wide), wide)
        total = acc[k, :, cols] + jnp.dot(
            xcat[k, :, pl.ds(half, half)], wbuf[m, pl.ds(half, half)], preferred_element_type=F32
        )
        hidden = gelu(total).astype(BF16)
        logits[k] = logits[k] + jnp.dot(hidden, headw[cols, :], preferred_element_type=F32)

    for copy in loads[:2]:
        copy.wait()
    for copy in halos:
        copy.wait()

    def first(i, carry):
        build(i % 2, i // 2)
        return carry

    lax.fori_loop(0, 4, first, 0)

    def step(j, carry):
        @pl.when(j < units)
        def _():
            x_copy(j).wait_recv()
            y_copy(cx, j).start()

            @pl.when(y == 0)
            def _():
                z_copy(cx, j).start()

            m_copy(0, cx, j).start()

        @pl.when((j >= LAG) & (j < units + LAG))
        def _():
            y_copy(cy, j - LAG).wait_recv()

            @pl.when(y == 1)
            def _():
                z_copy(cy, j - LAG).start()

            m_copy(1, cy, j - LAG).start()

        @pl.when((j >= 2 * LAG) & (j < units + 2 * LAG))
        def _():
            z_copy(cz, j - 2 * LAG).wait_recv()
            m_copy(2, cz, j - 2 * LAG).start()

        @pl.when(j == 0)
        def _():
            lax.fori_loop(4, 8, first, 0)
            for copy in loads[2:]:
                copy.wait()
            for copy in own:
                copy.wait()

        pace = SPLIT // 2

        @pl.when((j >= 1) & ((j - 1) % pace == 0) & (j < units + 1))
        def _():
            i = (j - 1) // pace
            near(1 - i % 2, i // 2)

        late = j - SPLIT - 2 * LAG

        @pl.when((late >= 0) & (late % pace == 0))
        def _():
            k = 1 - late // pace % 2
            m = late // SPLIT

            @pl.when(k == 1)
            def _():
                for kind, color in enumerate((cx, cy, cz)):
                    for u in range(SPLIT):
                        m_copy(kind, color, SPLIT * m + u).wait_recv()

            remote_part(k, m)

        return carry

    lax.fori_loop(0, units + 2 * LAG + 1, step, 0)

    def t_copy(p):
        cols = pl.ds(p * wide, wide)
        return remote(sendt.at[:, cols], rev_out.at[:, cols], t_send.at[p], t_recv.at[p], {"seq": mirror})

    for p in range(pieces):
        cols = pl.ds(p * wide, wide)
        value = softplus(logits[1, :, cols]).astype(BF16)
        sendt[:, cols] = jnp.dot(flip[...], value, preferred_element_type=F32).astype(BF16)
        if p:
            t_copy(p - 1).start()
    remote_part(0, blocks - 1)
    t_copy(pieces - 1).start()
    keep = []
    for p in range(pieces):
        cols = pl.ds(p * wide, wide)
        keept[:, cols] = softplus(logits[0, :, cols]).astype(BF16)
        keep.append(pltpu.make_async_copy(keept.at[:, cols], fwd_out.at[:, cols], out_sem.at[p]))
        if p:
            keep[p - 1].start()

    def drain(j, carry):
        x_copy(j).wait_send()
        y_copy(cx, j).wait_send()
        z_copy(2 * z, j).wait_send()
        for kind, color in enumerate((cx, cy, cz)):
            m_copy(kind, color, j).wait_send()
        return carry

    lax.fori_loop(0, units, drain, 0)
    keep[-1].start()
    for copy in keep:
        copy.wait()
    for p in range(pieces):
        t_copy(p).wait()


def fused(forward_embed, reverse_embed, conv_weight, conv_bias, head_weight, head_bias):
    rows, channels = forward_embed.shape
    _, taps, depth, _ = conv_weight.shape
    tracks = head_weight.shape[1]
    blocks = channels // WIDE
    units = SPLIT * blocks
    pieces = tracks // WIDE
    dma = pltpu.SemaphoreType.DMA
    anywhere = pl.BlockSpec(memory_space=pl.ANY)
    vmem = pl.BlockSpec(memory_space=pltpu.VMEM)
    forward_tracks, reverse_tracks = pl.pallas_call(
        functools.partial(kernel, taps),
        out_shape=[jax.ShapeDtypeStruct((rows, tracks), BF16)] * 2,
        in_specs=[anywhere, anywhere, anywhere, vmem, anywhere, vmem],
        out_specs=[anywhere, anywhere],
        scratch_shapes=[
            pltpu.VMEM((2, rows, channels), BF16),
            pltpu.VMEM((2, 2, 16, channels), BF16),
            pltpu.VMEM((2, rows, 4 * taps * depth), BF16),
            pltpu.VMEM((blocks, 4 * taps * depth, WIDE), BF16),
            pltpu.VMEM((2, rows, channels), F32),
            pltpu.VMEM((channels, tracks), BF16),
            pltpu.VMEM((2, rows, tracks), F32),
            pltpu.VMEM((rows, rows), BF16),
            pltpu.VMEM((rows, tracks), BF16),
            pltpu.VMEM((rows, tracks), BF16),
            dma((3 + taps * blocks,)),
            dma((2, 2)), dma((2, 2)),
            dma((taps, blocks)), dma((taps, blocks)),
            dma((units,)), dma((units,)),
            dma((units,)), dma((units,)),
            dma((units,)), dma((units,)),
            dma((3, units)), dma((3, units)),
            dma((pieces,)), dma((pieces,)), dma((pieces,)),
        ],
        compiler_params=pltpu.CompilerParams(
            collective_id=0, has_side_effects=True, vmem_limit_bytes=62 * 1024 * 1024
        ),
    )(forward_embed, reverse_embed, conv_weight, conv_bias, head_weight, head_bias[None])
    return (0.5 * (forward_tracks.astype(F32) + reverse_tracks.astype(F32))).astype(BF16)


def with_halo(block, axis):
    count = lax.axis_size(axis)
    forward = [(i, i + 1) for i in range(count - 1)]
    backward = [(target, source) for source, target in forward]
    low = lax.ppermute(block[-1:], axis, forward)
    high = lax.ppermute(block[:1], axis, backward)
    return jnp.concatenate([low, block, high], axis=0)


def general(forward_embed, reverse_embed, conv_weight, conv_bias, head_weight, head_bias):
    count = lax.axis_size("seq")
    layers, taps = conv_weight.shape[:2]
    gathered = [lax.all_gather(conv_weight[n], "seq", axis=1, tiled=True) for n in range(layers)]

    def strand(hidden):
        for n in range(layers):
            rows = hidden.shape[0]
            padded = with_halo(hidden, "seq")
            total = sum(
                jnp.dot(padded[k : k + rows], gathered[n][k], preferred_element_type=F32) for k in range(taps)
            )
            hidden = jax.nn.gelu(total + conv_bias[n], approximate=False).astype(BF16)
        logits = jnp.dot(hidden, head_weight, preferred_element_type=F32) + head_bias
        return jax.nn.softplus(logits).astype(BF16)

    reverse_tracks = strand(reverse_embed)[::-1]
    reverse_tracks = lax.ppermute(reverse_tracks, "seq", [(i, count - 1 - i) for i in range(count)])
    mean = 0.5 * (strand(forward_embed).astype(F32) + reverse_tracks.astype(F32))
    return mean.astype(BF16)


def solution(mesh):
    cubes = mesh.shape["seq"] == 4 and mesh.shape["batch"] % 4 == 0
    return jax.shard_map(
        fused if cubes else general,
        mesh=mesh,
        in_specs=(
            P(("batch", "seq"), None),
            P(("batch", "seq"), None),
            P(None, None, "seq", None),
            P(),
            P(),
            P(),
        ),
        out_specs=P(("batch", "seq"), None),
        check_vma=False,
    )
```

time: 78.5 us -> 68.2 us (0.87); the launches traced: 77.2 us -> 67.9 us
  Pallas kernels: 75.1 us -> 65.4 us
  other arithmetic: 0 us -> 2.53 us
  local copies, waits for them, and re-layouts: 2.06 us -> 0 us
    pallas_call x1, Pallas kernels: 75.1 us -> 65.4 us  [fused(): pl.pallas_call(functools.partial(kernel, taps), out_shape=[jax.ShapeDtype...]
    convert_element_type x0 -> x1, other arithmetic: none -> 2.53 us  [fused(): (0.5 * (forward_tracks.astype(F32) + reverse_tracks.astype(F32))).astype(...]
    unnamed x1 -> x0, local copies, waits for them, and re-layouts: 2.06 us -> none
where the time goes in v2:
time: 68.2 us; the launch traced here: 67.9 us
  Pallas kernels  65.4 us (96%)
  other arithmetic  2.53 us (4%)
    pallas_call x1, Pallas kernels, fused(): pl.pallas_call(functools.partial(kernel, taps), out_shape=[jax.ShapeDtype...  65.4 us
    convert_element_type x1, other arithmetic, fused(): (0.5 * (forward_tracks.astype(F32) + reverse_tracks.astype(F32))).astype(...  2.53 us

profile of v2, /device:TPU:0, one launch (start us, length us, event | category | flops | bytes accessed | tf_op | source)
XLA Modules:
  0.0 67.9 jit_solution(17198096649349170855)
XLA Ops:
  0.0 65.4 %shard_map.64 = (bf16[384,1024]{1,0:T(8,128)(2,1)}, bf16[384,1024]{1,0:T(8,128)(2,1)}) custom-call(bf16[384,1536]{1,0:T(8,128)(2,1)} %fwd_hbm.1, bf16[384,1536]{1,0:T(8,128)(2,1)} %rev_hbm.1, bf16[1,3,384,1536]{3,2,1,0:T(8,128)(2,1)} %w_hbm.1, f32[1,1536]{1,0:T(1,128)} %cb_ref.1, bf16[1536,1024]{1,0:T(8,128)(2,1)} %hw_hbm.1, f32[1,1024]{1,0:T(1,128)} %bitcast.1), custom_call_target="tpu_custom_call" | custom-call | tf_op jit(solution)/shard_map/pallas_call | solution.py:282
  65.4 2.5 %multiply_convert_fusion = bf16[384,1024]{1,0:T(8,128)(2,1)} fusion(bf16[384,1024]{1,0:T(8,128)(2,1)} %get-tuple-element.8, bf16[384,1024]{1,0:T(8,128)(2,1)} %get-tuple-element.7), kind=kLoop, calls=%fused_computation | loop fusion | flops 1966080 | bytes 2359296 | tf_op jit(solution)/shard_map/convert_element_type | solution.py:311

commit v3 on v2

--- a/solution.py
+++ b/solution.py
@@ -28,9 +28,9 @@
 
 def kernel(
     taps, fwd_hbm, rev_hbm, w_hbm, cb_ref, hw_hbm, hb_ref, fwd_out, rev_out,
-    embed, halo, xcat, wbuf, acc, headw, logits, flip, sendt, keept,
+    embed, halo, guest, xcat, wbuf, acc, headw, logits, flip, sendt, keept,
     local_sem, halo_send, halo_recv, own_send, own_recv,
-    x_send, x_recv, y_send, y_recv, z_send, z_recv, m_send, m_recv, t_send, t_recv, out_sem,
+    x_send, x_recv, y_send, y_recv, z_send, z_recv, m_send, m_recv, t_send, t_recv, out_sem, guest_sem,
 ):
     s = lax.axis_index("seq")
     b = lax.axis_index("batch")
@@ -56,6 +56,8 @@
     half = 2 * taps * depth
     tracks = hb_ref.shape[1]
     pieces = tracks // wide
+    visit = guest.shape[0] - halo.shape[2]
+    kept = rows - visit
 
     barrier = pltpu.get_barrier_semaphore()
     for peer in ({"seq": mate}, {"seq": across}, {"seq": mirror}, {"batch": yp}, {"batch": zp}):
@@ -85,7 +87,8 @@
     halos = []
     for k, src in enumerate((fwd_hbm, rev_hbm)):
         halos.append(remote(src.at[pl.ds(rows - tile, tile)], halo.at[k, 0], halo_send.at[k, 0], halo_recv.at[k, 0], {"seq": (s + 1) % 4}))
-        halos.append(remote(src.at[pl.ds(0, tile)], halo.at[k, 1], halo_send.at[k, 1], halo_recv.at[k, 1], {"seq": (s + 3) % 4}))
+        target = (s + 3) % 4 if k == 0 else across
+        halos.append(remote(src.at[pl.ds(0, tile)], halo.at[k, 1], halo_send.at[k, 1], halo_recv.at[k, 1], {"seq": target}))
     for copy in halos:
         copy.start()
 
@@ -107,6 +110,9 @@
     def m_copy(kind, color, j):
         return remote(cell(2, color, j), cell(3, color, j), m_send.at[kind, j], m_recv.at[kind, j], {"seq": mate})
 
+    guests = remote(
+        rev_hbm.at[pl.ds(kept - tile, visit + tile)], guest, guest_sem.at[0], guest_sem.at[1], {"seq": mirror}
+    )
     own = [
         remote(
             w_hbm.at[0, k, :, pl.ds(m * wide, wide)], wbuf.at[m, pl.ds((taps + k) * depth, depth)],
@@ -132,8 +138,24 @@
 
     line = lax.broadcasted_iota(jnp.int32, (rows, depth), 0)
 
+    def shard_of(slot):
+        return (far + (slot // 2) * (1 - 2 * far)) * 2 + core + (slot % 2) * (1 - 2 * core)
+
+    def build_guest(slot, carry):
+        cols = pl.ds(pl.multiple_of(shard_of(slot) * depth, LANES), depth)
+        full = guest[:, cols].astype(F32)
+        high = jnp.where(s == 2, embed[1, pl.ds(0, tile), cols], halo[1, 1, :, cols]).astype(F32)[0:1]
+        high = jnp.where(s == 0, 0.0, high)
+        before = pltpu.roll(full, 1, 0)[tile:]
+        after = pltpu.roll(full, visit + tile - 1, 0)[tile:]
+        after = jnp.where(lax.broadcasted_iota(jnp.int32, (visit, depth), 0) == visit - 1, high, after)
+        for tap, value in enumerate((before, full[tile:], after)):
+            place = pl.ds(pl.multiple_of((slot * taps + tap) * depth, LANES), depth)
+            xcat[1, pl.ds(kept, visit), place] = value.astype(BF16)
+        return carry
+
     def build(k, slot):
-        shard = (s // 2 + (slot // 2) * (1 - 2 * far)) * 2 + core + (slot % 2) * (1 - 2 * core)
+        shard = shard_of(slot)
         cols = pl.ds(pl.multiple_of(shard * depth, LANES), depth)
         mid = embed[k, :, cols]
         wide_mid = mid.astype(F32)
@@ -148,18 +170,28 @@
 
     def near(k, m):
         cols = pl.ds(pl.multiple_of(m * wide, wide), wide)
-        acc[k, :, cols] = (
-            jnp.dot(xcat[k, :, pl.ds(0, half)], wbuf[m, pl.ds(0, half)], preferred_element_type=F32)
+        own_rows = pl.ds(0, kept if k else rows)
+        acc[k, own_rows, cols] = (
+            jnp.dot(xcat[k, own_rows, pl.ds(0, half)], wbuf[m, pl.ds(0, half)], preferred_element_type=F32)
             + cb_ref[:, cols]
         )
 
     def remote_part(k, m):
         cols = pl.ds(pl.multiple_of(m * wide, wide), wide)
-        total = acc[k, :, cols] + jnp.dot(
-            xcat[k, :, pl.ds(half, half)], wbuf[m, pl.ds(half, half)], preferred_element_type=F32
+        own_rows = pl.ds(0, kept if k else rows)
+        total = acc[k, own_rows, cols] + jnp.dot(
+            xcat[k, own_rows, pl.ds(half, half)], wbuf[m, pl.ds(half, half)], preferred_element_type=F32
         )
         hidden = gelu(total).astype(BF16)
-        logits[k] = logits[k] + jnp.dot(hidden, headw[cols, :], preferred_element_type=F32)
+        logits[k, own_rows] = logits[k, own_rows] + jnp.dot(hidden, headw[cols, :], preferred_element_type=F32)
+
+    def guest_part(m, carry):
+        cols = pl.ds(pl.multiple_of(m * wide, wide), wide)
+        part_rows = pl.ds(kept, visit)
+        total = jnp.dot(xcat[1, part_rows, :], wbuf[m], preferred_element_type=F32) + cb_ref[:, cols]
+        hidden = gelu(total).astype(BF16)
+        logits[1, part_rows] = logits[1, part_rows] + jnp.dot(hidden, headw[cols, :], preferred_element_type=F32)
+        return carry
 
     for copy in loads[:2]:
         copy.wait()
@@ -198,6 +230,10 @@
         def _():
             z_copy(cz, j - 2 * LAG).wait_recv()
             m_copy(2, cz, j - 2 * LAG).start()
+
+        @pl.when(j == units - 2)
+        def _():
+            guests.start()
 
         @pl.when(j == 0)
         def _():
@@ -212,7 +248,14 @@
         @pl.when((j >= 1) & ((j - 1) % pace == 0) & (j < units + 1))
         def _():
             i = (j - 1) // pace
-            near(1 - i % 2, i // 2)
+
+            @pl.when(i % 2 == 0)
+            def _():
+                near(1, i // 2)
+
+            @pl.when(i % 2 == 1)
+            def _():
+                near(0, i // 2)
 
         late = j - SPLIT - 2 * LAG
 
@@ -227,7 +270,11 @@
                     for u in range(SPLIT):
                         m_copy(kind, color, SPLIT * m + u).wait_recv()
 
-            remote_part(k, m)
+                remote_part(1, m)
+
+            @pl.when(k == 0)
+            def _():
+                remote_part(0, m)
 
         return carry
 
@@ -235,12 +282,13 @@
 
     def t_copy(p):
         cols = pl.ds(p * wide, wide)
-        return remote(sendt.at[:, cols], rev_out.at[:, cols], t_send.at[p], t_recv.at[p], {"seq": mirror})
+        return remote(sendt.at[pl.ds(0, kept), cols], rev_out.at[pl.ds(visit, kept), cols], t_send.at[p], t_recv.at[p], {"seq": mirror})
 
     for p in range(pieces):
         cols = pl.ds(p * wide, wide)
-        value = softplus(logits[1, :, cols]).astype(BF16)
-        sendt[:, cols] = jnp.dot(flip[...], value, preferred_element_type=F32).astype(BF16)
+        value = softplus(logits[1, pl.ds(0, kept), cols]).astype(BF16)
+        turn = flip[pl.ds(visit, kept), pl.ds(0, kept)]
+        sendt[pl.ds(0, kept), cols] = jnp.dot(turn, value, preferred_element_type=F32).astype(BF16)
         if p:
             t_copy(p - 1).start()
     remote_part(0, blocks - 1)
@@ -253,6 +301,15 @@
         if p:
             keep[p - 1].start()
 
+    guests.wait_recv()
+    keep[-1].start()
+    lax.fori_loop(0, 4, build_guest, 0)
+    lax.fori_loop(0, blocks, guest_part, 0)
+    value = softplus(logits[1, pl.ds(kept, visit)]).astype(BF16)
+    turn = flip[pl.ds(0, visit), pl.ds(kept, visit)]
+    sendt[pl.ds(kept, visit)] = jnp.dot(turn, value, preferred_element_type=F32).astype(BF16)
+    keep.append(pltpu.make_async_copy(sendt.at[pl.ds(kept, visit)], rev_out.at[pl.ds(0, visit)], out_sem.at[pieces]))
+
     def drain(j, carry):
         x_copy(j).wait_send()
         y_copy(cx, j).wait_send()
@@ -265,6 +322,7 @@
     keep[-1].start()
     for copy in keep:
         copy.wait()
+    guests.wait_send()
     for p in range(pieces):
         t_copy(p).wait()
 
@@ -287,6 +345,7 @@
         scratch_shapes=[
             pltpu.VMEM((2, rows, channels), BF16),
             pltpu.VMEM((2, 2, 16, channels), BF16),
+            pltpu.VMEM((rows // 2 + 16, channels), BF16),
             pltpu.VMEM((2, rows, 4 * taps * depth), BF16),
             pltpu.VMEM((blocks, 4 * taps * depth, WIDE), BF16),
             pltpu.VMEM((2, rows, channels), F32),
@@ -302,7 +361,7 @@
             dma((units,)), dma((units,)),
             dma((units,)), dma((units,)),
             dma((3, units)), dma((3, units)),
-            dma((pieces,)), dma((pieces,)), dma((pieces,)),
+            dma((pieces,)), dma((pieces,)), dma((pieces + 1,)), dma((2,)),
         ],
         compiler_params=pltpu.CompilerParams(
             collective_id=0, has_side_effects=True, vmem_limit_bytes=62 * 1024 * 1024

time: 68.2 us -> 60.8 us (0.89); the launches traced: 67.9 us -> 59.6 us
  Pallas kernels: 65.4 us -> 57.1 us
    pallas_call x1, Pallas kernels: 65.4 us -> 57.1 us  [fused(): pl.pallas_call(functools.partial(kernel, taps), out_shape=[jax.ShapeDtype...]
where the time goes in v3:
time: 60.8 us; the launch traced here: 59.6 us
  Pallas kernels  57.1 us (94%)
  other arithmetic  2.53 us (4%)
    pallas_call x1, Pallas kernels, fused(): pl.pallas_call(functools.partial(kernel, taps), out_shape=[jax.ShapeDtype...  57.1 us
    convert_element_type x1, other arithmetic, fused(): (0.5 * (forward_tracks.astype(F32) + reverse_tracks.astype(F32))).astype(...  2.53 us

profile of v3, /device:TPU:0, one launch (start us, length us, event | category | flops | bytes accessed | tf_op | source)
XLA Modules:
  0.0 59.6 jit_solution(13755412726411419494)
XLA Ops:
  0.0 57.1 %shard_map.64 = (bf16[384,1024]{1,0:T(8,128)(2,1)}, bf16[384,1024]{1,0:T(8,128)(2,1)}) custom-call(bf16[384,1536]{1,0:T(8,128)(2,1)} %fwd_hbm.1, bf16[384,1536]{1,0:T(8,128)(2,1)} %rev_hbm.1, bf16[1,3,384,1536]{3,2,1,0:T(8,128)(2,1)} %w_hbm.1, f32[1,1536]{1,0:T(1,128)} %cb_ref.1, bf16[1536,1024]{1,0:T(8,128)(2,1)} %hw_hbm.1, f32[1,1024]{1,0:T(1,128)} %bitcast.1), custom_call_target="tpu_custom_call" | custom-call | tf_op jit(solution)/shard_map/pallas_call | solution.py:340
  57.1 2.5 %multiply_convert_fusion = bf16[384,1024]{1,0:T(8,128)(2,1)} fusion(bf16[384,1024]{1,0:T(8,128)(2,1)} %get-tuple-element.8, bf16[384,1024]{1,0:T(8,128)(2,1)} %get-tuple-element.7), kind=kLoop, calls=%fused_computation | loop fusion | flops 1966080 | bytes 2359296 | tf_op jit(solution)/shard_map/convert_element_type | solution.py:370
